TPU v7x, 256 devices: a whole 4x4x8 slice. The times are simulated.
256 devices in a mesh: blk: 8 (over x_hi, y), group: 32 (over z, x_lo, core).
Axes of the slice: x: 4 (x_hi: 2, x_lo: 2; x = x_hi * 2 + x_lo), y: 4, z: 8, core: 2. Of those that a mesh axis runs over, the one named last changes fastest.
Arguments:
- walk_rows: bfloat16 [4096, 131072], P('blk', 'group'), may hold values from -6 to 6
- col_values: bfloat16 [49152, 4096], P('group', 'blk'), may hold values from -0.02734375 to 0.02734375
- col_index: int32 [96, 8], P('group'), may hold values from 0 to 7
- col_count: int32 [32, 8], P('group'), may hold values from 1 to 3, as said below
Outputs:
- inflated: float32 [4096, 4096], P(('blk', 'group'))
Inputs may be any that keep to these rules, and one draw needn't show every extreme that they name: `col_count`: each list holds 1 to 3 valid slots; some list holds 3; contents of the other slots are arbitrary.
All inputs are finite; a program needn't handle non-finite values.
Results may differ from a plain program's by a relative error of at most 0.0003.
Values may be sent and summed in bfloat16 or wider, within the bound.
No kernel may reach another device: no remote copies, remote signals or barrier semaphores. Data moves between devices by JAX's collectives and lax.ppermute only.
A program may use at most 64 MiB of HBM per device.

v0:
```python
import jax
import jax.numpy as jnp
from jax import lax
from jax.sharding import PartitionSpec as P


def shifted(shard, axis, by):
    size = lax.axis_size(axis)
    return lax.ppermute(shard, axis, [(i, (i + by) % size) for i in range(size)])


def on_device(walk_rows, col_values, col_index, col_count):
    width = col_values.shape[1]
    slots = col_values.shape[0] // width
    nblock = lax.axis_size("blk")
    myself = lax.axis_index("blk")
    rows_here = walk_rows.shape[0]
    share = rows_here // lax.axis_size("group")

    def panel_product(rows, values, panel):
        index = lax.dynamic_slice_in_dim(col_index, panel, 1, 1)[:, 0]
        count = lax.dynamic_slice_in_dim(col_count, panel, 1, 1)[0, 0]
        total = jnp.zeros((rows.shape[0], width), jnp.float32)
        for slot in range(slots):
            block = lax.dynamic_slice_in_dim(rows, index[slot] * width, width, 1)
            piece = values[slot * width : (slot + 1) * width]
            product = jnp.dot(block, piece, preferred_element_type=jnp.float32)
            total = total + jnp.where(slot < count, product, jnp.zeros_like(product))
        return total

    def turn(step, carry):
        values, result = carry
        panel = (myself - step) % nblock
        part = panel_product(walk_rows, values, panel)
        reduced = lax.psum_scatter(part, "group", scatter_dimension=0, tiled=True)
        result = lax.dynamic_update_slice_in_dim(result, reduced, panel * width, 1)
        values = shifted(values, "blk", 1)
        return (values, result)

    start_out = jnp.zeros((share, nblock * width), jnp.float32)
    unused, expanded = lax.fori_loop(0, nblock, turn, (col_values, start_out))
    squared = expanded * expanded
    column = jnp.sum(squared, axis=0)
    total = lax.psum(column, ("blk", "group"))
    scale = total / (nblock * rows_here) + 1e-06
    return squared / scale


def solution(mesh):
    return jax.shard_map(
        on_device,
        mesh=mesh,
        in_specs=(P("blk", "group"), P("group", "blk"), P("group", None), P("group", None)),
        out_specs=P(("blk", "group"), None),
        check_vma=False,
    )
```

profile of v0, /device:TPU:1, one launch (start us, length us, event | category | flops | bytes accessed | tf_op | source)
XLA Modules:
  0.0 1125.3 jit_solution(7067308069750690020)
XLA Ops:
  6.6 1.4 copy-done
  7.9 1030.1 %while.17 = (s32[]{:T(128)}, bf16[1536,512]{1,0:T(8,128)(2,1)S(1)}, f32[16,4096]{1,0:T(8,128)S(1)}, s32[]{:T(128)}, s32[1,8]{1,0:T(1,128)S(1)}, /*index=5*/s32[3...) while((s32[]{:T(128)}, bf16[1536,512]{1,0:T(8,128)(2,1)S(1)}, ...), condition=%wide.region_2.3_spmd, body=%wide.region_0.2_spmd.sunk | while | flops 806617088 | bytes 21137560 | solution.py:41
  8.1 0.6 fusion.28
  10.5 0.7 fusion.29
  12.4 2.1 convolution_select_fusion.5
  14.5 1.5 convolution_select_fusion.6
  16.0 2.5 fusion.30
  18.5 2.2 collective-permute-start
  20.7 117.8 %reduce-scatter.2.cloned.1.call-done = f32[16,512]{1,0:T(8,128)} async-done(((f32[512,512]{1,0:T(8,128)}), f32[16,512]{1,0:T(8,128)}) %reduce-scatter.2.cloned.1.call-update) | async-done | bytes 32784 | tf_op jit(solution)/shard_map/while/body/eval_jaxpr/reduce_scatter | solution.py:35
  138.5 0.8 constant_dynamic-update-slice_fusion.2
  139.4 0.6 fusion.28
  141.8 0.7 fusion.29
  143.7 2.1 convolution_select_fusion.5
  145.8 1.5 convolution_select_fusion.6
  147.3 2.5 fusion.30
  149.9 117.1 %reduce-scatter.2.cloned.1.call-done = f32[16,512]{1,0:T(8,128)} async-done(((f32[512,512]{1,0:T(8,128)}), f32[16,512]{1,0:T(8,128)}) %reduce-scatter.2.cloned.1.call-update) | async-done | bytes 32784 | tf_op jit(solution)/shard_map/while/body/eval_jaxpr/reduce_scatter | solution.py:35
  267.0 0.8 constant_dynamic-update-slice_fusion.2
  267.8 0.6 fusion.28
  270.3 0.7 fusion.29
  272.2 2.1 convolution_select_fusion.5
  274.3 1.5 convolution_select_fusion.6
  275.8 2.5 fusion.30
  278.4 116.7 %reduce-scatter.2.cloned.1.call-done = f32[16,512]{1,0:T(8,128)} async-done(((f32[512,512]{1,0:T(8,128)}), f32[16,512]{1,0:T(8,128)}) %reduce-scatter.2.cloned.1.call-update) | async-done | bytes 32784 | tf_op jit(solution)/shard_map/while/body/eval_jaxpr/reduce_scatter | solution.py:35
  395.1 0.8 constant_dynamic-update-slice_fusion.2
  396.0 0.6 fusion.28
  398.4 0.7 fusion.29
  400.4 2.1 convolution_select_fusion.5
  402.5 1.5 convolution_select_fusion.6
  404.0 2.5 fusion.30
  406.6 116.8 %reduce-scatter.2.cloned.1.call-done = f32[16,512]{1,0:T(8,128)} async-done(((f32[512,512]{1,0:T(8,128)}), f32[16,512]{1,0:T(8,128)}) %reduce-scatter.2.cloned.1.call-update) | async-done | bytes 32784 | tf_op jit(solution)/shard_map/while/body/eval_jaxpr/reduce_scatter | solution.py:35
  523.4 0.8 constant_dynamic-update-slice_fusion.2
  524.3 0.6 fusion.28
  526.8 0.7 fusion.29
  528.7 2.1 convolution_select_fusion.5
  530.8 1.5 convolution_select_fusion.6
  532.3 2.5 fusion.30
  535.0 116.8 %reduce-scatter.2.cloned.1.call-done = f32[16,512]{1,0:T(8,128)} async-done(((f32[512,512]{1,0:T(8,128)}), f32[16,512]{1,0:T(8,128)}) %reduce-scatter.2.cloned.1.call-update) | async-done | bytes 32784 | tf_op jit(solution)/shard_map/while/body/eval_jaxpr/reduce_scatter | solution.py:35
  651.9 0.8 constant_dynamic-update-slice_fusion.2
  652.7 0.6 fusion.28
  655.2 0.7 fusion.29
  657.1 2.1 convolution_select_fusion.5
  659.2 1.5 convolution_select_fusion.6
  660.7 2.5 fusion.30
  663.2 0.3 collective-permute-start
  663.5 116.9 %reduce-scatter.2.cloned.1.call-done = f32[16,512]{1,0:T(8,128)} async-done(((f32[512,512]{1,0:T(8,128)}), f32[16,512]{1,0:T(8,128)}) %reduce-scatter.2.cloned.1.call-update) | async-done | bytes 32784 | tf_op jit(solution)/shard_map/while/body/eval_jaxpr/reduce_scatter | solution.py:35
  780.3 0.8 constant_dynamic-update-slice_fusion.2
  781.2 0.6 fusion.28
  783.7 0.7 fusion.29
  785.6 2.1 convolution_select_fusion.5
  787.7 1.5 convolution_select_fusion.6
  789.2 2.5 fusion.30
  791.7 0.3 collective-permute-start
  791.9 116.9 %reduce-scatter.2.cloned.1.call-done = f32[16,512]{1,0:T(8,128)} async-done(((f32[512,512]{1,0:T(8,128)}), f32[16,512]{1,0:T(8,128)}) %reduce-scatter.2.cloned.1.call-update) | async-done | bytes 32784 | tf_op jit(solution)/shard_map/while/body/eval_jaxpr/reduce_scatter | solution.py:35
  908.8 0.8 constant_dynamic-update-slice_fusion.2
  909.7 0.6 fusion.28
  912.1 0.7 fusion.29
  914.0 2.1 convolution_select_fusion.5
  916.1 1.5 convolution_select_fusion.6
  917.6 2.5 fusion.30
  920.1 0.5 collective-permute-start
  920.6 116.6 %reduce-scatter.2.cloned.1.call-done = f32[16,512]{1,0:T(8,128)} async-done(((f32[512,512]{1,0:T(8,128)}), f32[16,512]{1,0:T(8,128)}) %reduce-scatter.2.cloned.1.call-update) | async-done | bytes 32784 | tf_op jit(solution)/shard_map/while/body/eval_jaxpr/reduce_scatter | solution.py:35
  1037.3 0.8 constant_dynamic-update-slice_fusion.2
  1038.1 79.7 %psum.7 = f32[4096]{0:T(1024)S(1)} all-reduce(f32[4096]{0:T(1024)S(1)} %multiply_reduce_fusion), channel_id=1, replica_groups=mesh['blk'=8,'group'=32] {'blk','group'}, use_global_device_ids=true, to_apply=%region_4.5 | all-reduce | flops 4096 | bytes 32768 | tf_op jit(solution)/shard_map/psum | solution.py:44
  1117.7 0.7 multiply_divide_fusion
  (52 shorter events, 2.3 us)
Async XLA Ops:
  6.5 1.4 copy-start
  6.5 1.4 copy-start.1
  6.5 1.4 copy-start.2
  7.9 130.5 %reduce-scatter.2.cloned.1.call-start = ((), (), s32[]{:S(2)}) async-start(), calls=%async_computation.1 | async-start | bytes 1081344 | tf_op jit(solution)/shard_map/while/body/eval_jaxpr/reduce_scatter | solution.py:35
  18.5 120.8 %collective-permute-start = (bf16[1536,512]{1,0:T(8,128)(2,1)S(1)}, bf16[1536,512]{1,0:T(8,128)(2,1)S(1)}, u32[]{:S(2)}, u32[]{:S(2)}) collective-permute-start(bf16[1536,512]{1,0:T(8,128)(2,1)S(1)} %copy.10), channel_id=1, source_target_pairs={{0,32},{32,64},{64,96},{96,128},{128,160},{160,192},{192,224},{224... | collective-permute-start | bytes 4718600 | tf_op jit(solution)/shard_map/while/body/eval_jaxpr/ppermute | solution.py:9
  139.3 127.7 %reduce-scatter.2.cloned.1.call-start = ((), (), s32[]{:S(2)}) async-start(), calls=%async_computation.1 | async-start | bytes 1081344 | tf_op jit(solution)/shard_map/while/body/eval_jaxpr/reduce_scatter | solution.py:35
  149.8 117.9 %collective-permute-start = (bf16[1536,512]{1,0:T(8,128)(2,1)S(1)}, bf16[1536,512]{1,0:T(8,128)(2,1)S(1)}, u32[]{:S(2)}, u32[]{:S(2)}) collective-permute-start(bf16[1536,512]{1,0:T(8,128)(2,1)S(1)} %copy.10), channel_id=1, source_target_pairs={{0,32},{32,64},{64,96},{96,128},{128,160},{160,192},{192,224},{224... | collective-permute-start | bytes 4718600 | tf_op jit(solution)/shard_map/while/body/eval_jaxpr/ppermute | solution.py:9
  267.7 127.4 %reduce-scatter.2.cloned.1.call-start = ((), (), s32[]{:S(2)}) async-start(), calls=%async_computation.1 | async-start | bytes 1081344 | tf_op jit(solution)/shard_map/while/body/eval_jaxpr/reduce_scatter | solution.py:35
  278.3 117.6 %collective-permute-start = (bf16[1536,512]{1,0:T(8,128)(2,1)S(1)}, bf16[1536,512]{1,0:T(8,128)(2,1)S(1)}, u32[]{:S(2)}, u32[]{:S(2)}) collective-permute-start(bf16[1536,512]{1,0:T(8,128)(2,1)S(1)} %copy.10), channel_id=1, source_target_pairs={{0,32},{32,64},{64,96},{96,128},{128,160},{160,192},{192,224},{224... | collective-permute-start | bytes 4718600 | tf_op jit(solution)/shard_map/while/body/eval_jaxpr/ppermute | solution.py:9
  395.9 127.5 %reduce-scatter.2.cloned.1.call-start = ((), (), s32[]{:S(2)}) async-start(), calls=%async_computation.1 | async-start | bytes 1081344 | tf_op jit(solution)/shard_map/while/body/eval_jaxpr/reduce_scatter | solution.py:35
  406.4 117.8 %collective-permute-start = (bf16[1536,512]{1,0:T(8,128)(2,1)S(1)}, bf16[1536,512]{1,0:T(8,128)(2,1)S(1)}, u32[]{:S(2)}, u32[]{:S(2)}) collective-permute-start(bf16[1536,512]{1,0:T(8,128)(2,1)S(1)} %copy.10), channel_id=1, source_target_pairs={{0,32},{32,64},{64,96},{96,128},{128,160},{160,192},{192,224},{224... | collective-permute-start | bytes 4718600 | tf_op jit(solution)/shard_map/while/body/eval_jaxpr/ppermute | solution.py:9
  524.2 127.7 %reduce-scatter.2.cloned.1.call-start = ((), (), s32[]{:S(2)}) async-start(), calls=%async_computation.1 | async-start | bytes 1081344 | tf_op jit(solution)/shard_map/while/body/eval_jaxpr/reduce_scatter | solution.py:35
  534.8 117.9 %collective-permute-start = (bf16[1536,512]{1,0:T(8,128)(2,1)S(1)}, bf16[1536,512]{1,0:T(8,128)(2,1)S(1)}, u32[]{:S(2)}, u32[]{:S(2)}) collective-permute-start(bf16[1536,512]{1,0:T(8,128)(2,1)S(1)} %copy.10), channel_id=1, source_target_pairs={{0,32},{32,64},{64,96},{96,128},{128,160},{160,192},{192,224},{224... | collective-permute-start | bytes 4718600 | tf_op jit(solution)/shard_map/while/body/eval_jaxpr/ppermute | solution.py:9
  652.6 127.7 %reduce-scatter.2.cloned.1.call-start = ((), (), s32[]{:S(2)}) async-start(), calls=%async_computation.1 | async-start | bytes 1081344 | tf_op jit(solution)/shard_map/while/body/eval_jaxpr/reduce_scatter | solution.py:35
  663.2 117.9 %collective-permute-start = (bf16[1536,512]{1,0:T(8,128)(2,1)S(1)}, bf16[1536,512]{1,0:T(8,128)(2,1)S(1)}, u32[]{:S(2)}, u32[]{:S(2)}) collective-permute-start(bf16[1536,512]{1,0:T(8,128)(2,1)S(1)} %copy.10), channel_id=1, source_target_pairs={{0,32},{32,64},{64,96},{96,128},{128,160},{160,192},{192,224},{224... | collective-permute-start | bytes 4718600 | tf_op jit(solution)/shard_map/while/body/eval_jaxpr/ppermute | solution.py:9
  781.1 127.7 %reduce-scatter.2.cloned.1.call-start = ((), (), s32[]{:S(2)}) async-start(), calls=%async_computation.1 | async-start | bytes 1081344 | tf_op jit(solution)/shard_map/while/body/eval_jaxpr/reduce_scatter | solution.py:35
  791.7 117.9 %collective-permute-start = (bf16[1536,512]{1,0:T(8,128)(2,1)S(1)}, bf16[1536,512]{1,0:T(8,128)(2,1)S(1)}, u32[]{:S(2)}, u32[]{:S(2)}) collective-permute-start(bf16[1536,512]{1,0:T(8,128)(2,1)S(1)} %copy.10), channel_id=1, source_target_pairs={{0,32},{32,64},{64,96},{96,128},{128,160},{160,192},{192,224},{224... | collective-permute-start | bytes 4718600 | tf_op jit(solution)/shard_map/while/body/eval_jaxpr/ppermute | solution.py:9
  909.6 127.7 %reduce-scatter.2.cloned.1.call-start = ((), (), s32[]{:S(2)}) async-start(), calls=%async_computation.1 | async-start | bytes 1081344 | tf_op jit(solution)/shard_map/while/body/eval_jaxpr/reduce_scatter | solution.py:35
  920.1 117.9 %collective-permute-start = (bf16[1536,512]{1,0:T(8,128)(2,1)S(1)}, bf16[1536,512]{1,0:T(8,128)(2,1)S(1)}, u32[]{:S(2)}, u32[]{:S(2)}) collective-permute-start(bf16[1536,512]{1,0:T(8,128)(2,1)S(1)} %copy.10), channel_id=1, source_target_pairs={{0,32},{32,64},{64,96},{96,128},{128,160},{160,192},{192,224},{224... | collective-permute-start | bytes 4718600 | tf_op jit(solution)/shard_map/while/body/eval_jaxpr/ppermute | solution.py:9
Sparse Core Ops, SparseCore 0:
  18.6 119.8 reduce-scatter.1
  149.9 116.9 reduce-scatter.1
  278.4 116.6 reduce-scatter.1
  406.6 116.8 reduce-scatter.1
  534.9 116.9 reduce-scatter.1
  663.3 116.9 reduce-scatter.1
  791.8 116.9 reduce-scatter.1
  920.2 116.9 reduce-scatter.1
where the time goes:
time: 1130 us
  waiting for transfers between devices  936 us (83%)
  blocking collectives  79.7 us (7%)
  matrix products  48.4 us (4%)
  loops' own time  24.6 us (2%)
  local copies, waits for them, and re-layouts  13.6 us (1%)
  between operations  13.4 us (1%)
    reduce_scatter x8, waiting for transfers between devices, turn(): reduced = lax.psum_scatter(part, 'group', scatter_dimension=0, tiled=True)  936 us
    psum x1, blocking collectives, on_device(): total = lax.psum(column, ('blk', 'group'))  79.7 us
    dot_general x24, matrix products, panel_product(): product = jnp.dot(block, piece, preferred_element_type=jnp.float32)  48.4 us
    another operation x1, loops' own time, on_device(): unused, expanded = lax.fori_loop(0, nblock, turn, (col_values, start_out))  24.6 us
  transfers between devices with their start and end apart: 16, of which 8 were waited for; matrix products, arithmetic and copies ran while one was open for 1% of the time, Pallas kernels for 0%

commit v1 on v0

--- a/solution.py
+++ b/solution.py
@@ -2,6 +2,7 @@
 import jax.numpy as jnp
 from jax import lax
 from jax.sharding import PartitionSpec as P
+from jax.lax import all_gather
 
 
 def shifted(shard, axis, by):
@@ -41,7 +42,12 @@
     unused, expanded = lax.fori_loop(0, nblock, turn, (col_values, start_out))
     squared = expanded * expanded
     column = jnp.sum(squared, axis=0)
-    total = lax.psum(column, ("blk", "group"))
+
+    def _convert_joints(matrix):
+        vec_out = jnp.sum(all_gather(matrix, ("blk", "group")), axis=0)
+        return vec_out
+
+    total = _convert_joints(column)
     scale = total / (nblock * rows_here) + 1e-06
     return squared / scale
 

time: 1130 us -> 1480 us (1.31)
  waiting for transfers between devices: 936 us -> 1360 us
  blocking collectives: 79.7 us -> 0 us
    all_gather x0 -> x1, waiting for transfers between devices: none -> 419 us  [_convert_joints(): vec_out = jnp.sum(all_gather(matrix, ('blk', 'group')), axis=0)]
    psum x1 -> x0, blocking collectives: 79.7 us -> none  [on_device(): total = lax.psum(column, ('blk', 'group'))]
  transfers between devices with their start and end apart: 16 -> 17, of which waited for: 8 -> 9; matrix products, arithmetic and copies ran while one was open for 1% -> 0% of each run, Pallas kernels for 0% -> 0%
where the time goes in v1:
time: 1480 us
  waiting for transfers between devices  1360 us (92%)
  matrix products  48.3 us (3%)
  loops' own time  26.2 us (2%)
  local copies, waits for them, and re-layouts  18.7 us (1%)
  between operations  14.8 us (1%)
    reduce_scatter x8, waiting for transfers between devices, turn(): reduced = lax.psum_scatter(part, 'group', scatter_dimension=0, tiled=True)  936 us
    all_gather x1, waiting for transfers between devices, _convert_joints(): vec_out = jnp.sum(all_gather(matrix, ('blk', 'group')), axis=0)  419 us
    dot_general x24, matrix products, panel_product(): product = jnp.dot(block, piece, preferred_element_type=jnp.float32)  48.3 us
  transfers between devices with their start and end apart: 17, of which 9 were waited for; matrix products, arithmetic and copies ran while one was open for 0% of the time, Pallas kernels for 0%

profile of v1, /device:TPU:1, one launch (start us, length us, event | category | flops | bytes accessed | tf_op | source)
XLA Modules:
  0.0 1475.7 jit_solution(11046664849335865723)
XLA Ops:
  7.4 1.4 copy-done
  8.8 1031.8 %while.17 = (s32[]{:T(128)}, bf16[1536,512]{1,0:T(8,128)(2,1)S(1)}, f32[16,4096]{1,0:T(8,128)S(1)}, s32[]{:T(128)}, s32[1,8]{1,0:T(1,128)S(1)}, /*index=5*/s32[3...) while((s32[]{:T(128)}, bf16[1536,512]{1,0:T(8,128)(2,1)S(1)}, ...), condition=%wide.region_2.3_spmd, body=%wide.region_0.2_spmd.sunk | while | flops 806617088 | bytes 21137560 | solution.py:42
  8.9 0.6 fusion.28
  11.3 0.7 fusion.29
  13.5 2.1 convolution_select_fusion.5
  15.6 1.5 convolution_select_fusion.6
  17.1 2.5 fusion.30
  19.5 2.2 collective-permute-start
  21.7 117.8 %reduce-scatter.2.cloned.1.call-done = f32[16,512]{1,0:T(8,128)} async-done(((f32[512,512]{1,0:T(8,128)}), f32[16,512]{1,0:T(8,128)}) %reduce-scatter.2.cloned.1.call-update) | async-done | bytes 32784 | tf_op jit(solution)/shard_map/while/body/eval_jaxpr/reduce_scatter | solution.py:36
  139.5 0.8 constant_dynamic-update-slice_fusion.2
  140.4 0.6 fusion.28
  142.8 0.7 fusion.29
  145.0 2.1 convolution_select_fusion.5
  147.1 1.5 convolution_select_fusion.6
  148.6 2.5 fusion.30
  151.1 116.8 %reduce-scatter.2.cloned.1.call-done = f32[16,512]{1,0:T(8,128)} async-done(((f32[512,512]{1,0:T(8,128)}), f32[16,512]{1,0:T(8,128)}) %reduce-scatter.2.cloned.1.call-update) | async-done | bytes 32784 | tf_op jit(solution)/shard_map/while/body/eval_jaxpr/reduce_scatter | solution.py:36
  268.0 0.8 constant_dynamic-update-slice_fusion.2
  268.9 0.6 fusion.28
  271.3 0.7 fusion.29
  273.4 2.1 convolution_select_fusion.5
  275.5 1.5 convolution_select_fusion.6
  277.0 2.5 fusion.30
  279.6 117.0 %reduce-scatter.2.cloned.1.call-done = f32[16,512]{1,0:T(8,128)} async-done(((f32[512,512]{1,0:T(8,128)}), f32[16,512]{1,0:T(8,128)}) %reduce-scatter.2.cloned.1.call-update) | async-done | bytes 32784 | tf_op jit(solution)/shard_map/while/body/eval_jaxpr/reduce_scatter | solution.py:36
  396.6 0.8 constant_dynamic-update-slice_fusion.2
  397.5 0.6 fusion.28
  399.9 0.7 fusion.29
  402.1 2.1 convolution_select_fusion.5
  404.2 1.5 convolution_select_fusion.6
  405.7 2.5 fusion.30
  408.3 116.9 %reduce-scatter.2.cloned.1.call-done = f32[16,512]{1,0:T(8,128)} async-done(((f32[512,512]{1,0:T(8,128)}), f32[16,512]{1,0:T(8,128)}) %reduce-scatter.2.cloned.1.call-update) | async-done | bytes 32784 | tf_op jit(solution)/shard_map/while/body/eval_jaxpr/reduce_scatter | solution.py:36
  525.2 0.8 constant_dynamic-update-slice_fusion.2
  526.1 0.6 fusion.28
  528.5 0.7 fusion.29
  530.7 2.1 convolution_select_fusion.5
  532.8 1.5 convolution_select_fusion.6
  534.2 2.5 fusion.30
  536.9 116.9 %reduce-scatter.2.cloned.1.call-done = f32[16,512]{1,0:T(8,128)} async-done(((f32[512,512]{1,0:T(8,128)}), f32[16,512]{1,0:T(8,128)}) %reduce-scatter.2.cloned.1.call-update) | async-done | bytes 32784 | tf_op jit(solution)/shard_map/while/body/eval_jaxpr/reduce_scatter | solution.py:36
  653.8 0.8 constant_dynamic-update-slice_fusion.2
  654.6 0.6 fusion.28
  657.1 0.7 fusion.29
  659.2 2.1 convolution_select_fusion.5
  661.3 1.5 convolution_select_fusion.6
  662.8 2.5 fusion.30
  665.5 117.0 %reduce-scatter.2.cloned.1.call-done = f32[16,512]{1,0:T(8,128)} async-done(((f32[512,512]{1,0:T(8,128)}), f32[16,512]{1,0:T(8,128)}) %reduce-scatter.2.cloned.1.call-update) | async-done | bytes 32784 | tf_op jit(solution)/shard_map/while/body/eval_jaxpr/reduce_scatter | solution.py:36
  782.6 0.8 constant_dynamic-update-slice_fusion.2
  783.4 0.6 fusion.28
  785.9 0.7 fusion.29
  788.0 2.1 convolution_select_fusion.5
  790.1 1.5 convolution_select_fusion.6
  791.6 2.5 fusion.30
  794.5 116.7 %reduce-scatter.2.cloned.1.call-done = f32[16,512]{1,0:T(8,128)} async-done(((f32[512,512]{1,0:T(8,128)}), f32[16,512]{1,0:T(8,128)}) %reduce-scatter.2.cloned.1.call-update) | async-done | bytes 32784 | tf_op jit(solution)/shard_map/while/body/eval_jaxpr/reduce_scatter | solution.py:36
  911.2 0.8 constant_dynamic-update-slice_fusion.2
  912.1 0.6 fusion.28
  914.5 0.7 fusion.29
  916.7 2.1 convolution_select_fusion.5
  918.8 1.5 convolution_select_fusion.6
  920.3 2.5 fusion.30
  922.8 117.0 %reduce-scatter.2.cloned.1.call-done = f32[16,512]{1,0:T(8,128)} async-done(((f32[512,512]{1,0:T(8,128)}), f32[16,512]{1,0:T(8,128)}) %reduce-scatter.2.cloned.1.call-update) | async-done | bytes 32784 | tf_op jit(solution)/shard_map/while/body/eval_jaxpr/reduce_scatter | solution.py:36
  1039.9 0.8 constant_dynamic-update-slice_fusion.2
  1040.7 0.7 multiply_reduce_fusion
  1041.3 418.8 %all-gather.3.cloned.1.call-done = f32[1048576]{0:T(1024)} async-done(((f32[4096]{0:T(1024)}), f32[1048576]{0:T(1024)}) %all-gather.3.cloned.1.call-update) | async-done | bytes 4194320 | tf_op jit(solution)/shard_map/all_gather | solution.py:47
  1460.1 5.0 reshape.22
  1465.1 2.4 reduce_sum.19
  1467.5 0.7 multiply_divide_fusion
  (56 shorter events, 2.9 us)
Async XLA Ops:
  7.4 1.4 copy-start
  7.4 1.4 copy-start.1
  7.4 1.4 copy-start.2
  8.8 130.7 %reduce-scatter.2.cloned.1.call-start = ((), (), s32[]{:S(2)}) async-start(), calls=%async_computation.2 | async-start | bytes 1081344 | tf_op jit(solution)/shard_map/while/body/eval_jaxpr/reduce_scatter | solution.py:36
  19.5 120.8 %collective-permute-start = (bf16[1536,512]{1,0:T(8,128)(2,1)S(1)}, bf16[1536,512]{1,0:T(8,128)(2,1)S(1)}, u32[]{:S(2)}, u32[]{:S(2)}) collective-permute-start(bf16[1536,512]{1,0:T(8,128)(2,1)S(1)} %copy.10), channel_id=1, source_target_pairs={{0,32},{32,64},{64,96},{96,128},{128,160},{160,192},{192,224},{224... | collective-permute-start | bytes 4718600 | tf_op jit(solution)/shard_map/while/body/eval_jaxpr/ppermute | solution.py:10
  140.3 127.7 %reduce-scatter.2.cloned.1.call-start = ((), (), s32[]{:S(2)}) async-start(), calls=%async_computation.2 | async-start | bytes 1081344 | tf_op jit(solution)/shard_map/while/body/eval_jaxpr/reduce_scatter | solution.py:36
  151.0 117.7 %collective-permute-start = (bf16[1536,512]{1,0:T(8,128)(2,1)S(1)}, bf16[1536,512]{1,0:T(8,128)(2,1)S(1)}, u32[]{:S(2)}, u32[]{:S(2)}) collective-permute-start(bf16[1536,512]{1,0:T(8,128)(2,1)S(1)} %copy.10), channel_id=1, source_target_pairs={{0,32},{32,64},{64,96},{96,128},{128,160},{160,192},{192,224},{224... | collective-permute-start | bytes 4718600 | tf_op jit(solution)/shard_map/while/body/eval_jaxpr/ppermute | solution.py:10
  268.7 127.9 %reduce-scatter.2.cloned.1.call-start = ((), (), s32[]{:S(2)}) async-start(), calls=%async_computation.2 | async-start | bytes 1081344 | tf_op jit(solution)/shard_map/while/body/eval_jaxpr/reduce_scatter | solution.py:36
  279.5 117.9 %collective-permute-start = (bf16[1536,512]{1,0:T(8,128)(2,1)S(1)}, bf16[1536,512]{1,0:T(8,128)(2,1)S(1)}, u32[]{:S(2)}, u32[]{:S(2)}) collective-permute-start(bf16[1536,512]{1,0:T(8,128)(2,1)S(1)} %copy.10), channel_id=1, source_target_pairs={{0,32},{32,64},{64,96},{96,128},{128,160},{160,192},{192,224},{224... | collective-permute-start | bytes 4718600 | tf_op jit(solution)/shard_map/while/body/eval_jaxpr/ppermute | solution.py:10
  397.4 127.8 %reduce-scatter.2.cloned.1.call-start = ((), (), s32[]{:S(2)}) async-start(), calls=%async_computation.2 | async-start | bytes 1081344 | tf_op jit(solution)/shard_map/while/body/eval_jaxpr/reduce_scatter | solution.py:36
  408.2 117.8 %collective-permute-start = (bf16[1536,512]{1,0:T(8,128)(2,1)S(1)}, bf16[1536,512]{1,0:T(8,128)(2,1)S(1)}, u32[]{:S(2)}, u32[]{:S(2)}) collective-permute-start(bf16[1536,512]{1,0:T(8,128)(2,1)S(1)} %copy.10), channel_id=1, source_target_pairs={{0,32},{32,64},{64,96},{96,128},{128,160},{160,192},{192,224},{224... | collective-permute-start | bytes 4718600 | tf_op jit(solution)/shard_map/while/body/eval_jaxpr/ppermute | solution.py:10
  526.0 127.8 %reduce-scatter.2.cloned.1.call-start = ((), (), s32[]{:S(2)}) async-start(), calls=%async_computation.2 | async-start | bytes 1081344 | tf_op jit(solution)/shard_map/while/body/eval_jaxpr/reduce_scatter | solution.py:36
  536.7 117.8 %collective-permute-start = (bf16[1536,512]{1,0:T(8,128)(2,1)S(1)}, bf16[1536,512]{1,0:T(8,128)(2,1)S(1)}, u32[]{:S(2)}, u32[]{:S(2)}) collective-permute-start(bf16[1536,512]{1,0:T(8,128)(2,1)S(1)} %copy.10), channel_id=1, source_target_pairs={{0,32},{32,64},{64,96},{96,128},{128,160},{160,192},{192,224},{224... | collective-permute-start | bytes 4718600 | tf_op jit(solution)/shard_map/while/body/eval_jaxpr/ppermute | solution.py:10
  654.5 128.0 %reduce-scatter.2.cloned.1.call-start = ((), (), s32[]{:S(2)}) async-start(), calls=%async_computation.2 | async-start | bytes 1081344 | tf_op jit(solution)/shard_map/while/body/eval_jaxpr/reduce_scatter | solution.py:36
  665.3 118.0 %collective-permute-start = (bf16[1536,512]{1,0:T(8,128)(2,1)S(1)}, bf16[1536,512]{1,0:T(8,128)(2,1)S(1)}, u32[]{:S(2)}, u32[]{:S(2)}) collective-permute-start(bf16[1536,512]{1,0:T(8,128)(2,1)S(1)} %copy.10), channel_id=1, source_target_pairs={{0,32},{32,64},{64,96},{96,128},{128,160},{160,192},{192,224},{224... | collective-permute-start | bytes 4718600 | tf_op jit(solution)/shard_map/while/body/eval_jaxpr/ppermute | solution.py:10
  783.3 127.9 %reduce-scatter.2.cloned.1.call-start = ((), (), s32[]{:S(2)}) async-start(), calls=%async_computation.2 | async-start | bytes 1081344 | tf_op jit(solution)/shard_map/while/body/eval_jaxpr/reduce_scatter | solution.py:36
  794.1 117.9 %collective-permute-start = (bf16[1536,512]{1,0:T(8,128)(2,1)S(1)}, bf16[1536,512]{1,0:T(8,128)(2,1)S(1)}, u32[]{:S(2)}, u32[]{:S(2)}) collective-permute-start(bf16[1536,512]{1,0:T(8,128)(2,1)S(1)} %copy.10), channel_id=1, source_target_pairs={{0,32},{32,64},{64,96},{96,128},{128,160},{160,192},{192,224},{224... | collective-permute-start | bytes 4718600 | tf_op jit(solution)/shard_map/while/body/eval_jaxpr/ppermute | solution.py:10
  912.0 127.9 %reduce-scatter.2.cloned.1.call-start = ((), (), s32[]{:S(2)}) async-start(), calls=%async_computation.2 | async-start | bytes 1081344 | tf_op jit(solution)/shard_map/while/body/eval_jaxpr/reduce_scatter | solution.py:36
  922.7 117.9 %collective-permute-start = (bf16[1536,512]{1,0:T(8,128)(2,1)S(1)}, bf16[1536,512]{1,0:T(8,128)(2,1)S(1)}, u32[]{:S(2)}, u32[]{:S(2)}) collective-permute-start(bf16[1536,512]{1,0:T(8,128)(2,1)S(1)} %copy.10), channel_id=1, source_target_pairs={{0,32},{32,64},{64,96},{96,128},{128,160},{160,192},{192,224},{224... | collective-permute-start | bytes 4718600 | tf_op jit(solution)/shard_map/while/body/eval_jaxpr/ppermute | solution.py:10
  1040.6 419.5 %all-gather.3.cloned.1.call-start = ((), (), s32[]{:S(2)}) async-start(), calls=%async_computation.1 | async-start | bytes 4210688 | tf_op jit(solution)/shard_map/all_gather | solution.py:47
Sparse Core Ops, SparseCore 0:
  19.7 119.8 reduce-scatter.1
  151.2 116.7 reduce-scatter.1
  279.6 116.9 reduce-scatter.1
  408.3 116.8 reduce-scatter.1
  536.8 116.8 reduce-scatter.1
  665.4 117.1 reduce-scatter.1
  794.2 116.9 reduce-scatter.1
  922.9 116.9 reduce-scatter.1
Sparse Core Ops, SparseCore 1:
  1043.0 417.1 all-gather.2
